TPU v7x, 32 devices: a whole 2x2x4 slice. The times are simulated.
32 devices in a mesh: sub: 8 (over z, y), col: 4 (over x, core).
Axes of the slice: x: 2, y: 2, z: 4, core: 2. Of those that a mesh axis runs over, the one named last changes fastest.
Arguments:
- rhs: bfloat16 [32, 1024, 128], P(('sub', 'col')), may hold values from -64 to 64
- schur: bfloat16 [32, 1024, 1024], P(('sub', 'col')), may hold values from -1 to 3
- local_inverse: bfloat16 [32, 1024, 1024], P(('sub', 'col')), may hold values from -1 to 2
- basis: bfloat16 [32, 8, 1024], P(('sub', 'col')), may hold values from -0.75 to 0.75
- coarse_inverse: bfloat16 [256, 256], P('sub', 'col'), may hold values from -1 to 2
- primal_index: int32 [32, 8], P(('sub', 'col')), may hold values from 0 to 255, as said below
- neighbour_dof: int32 [32, 1024], P(('sub', 'col')), may hold values from 0 to 1023, as said below
Outputs:
- solution: bfloat16 [32, 1024, 128], P(('sub', 'col'))
Inputs may be any that keep to these rules, and one draw needn't show every extreme that they name: `neighbour_dof`: each subdomain's unknowns in one shared block name places in the neighbour's facing block (for [0, 256) the neighbour's [256, 512), and so on), and the neighbour's entry names the place back. `primal_index`: every coarse unknown is named exactly once over all subdomains.
All inputs are finite; a program needn't handle non-finite values.
Results may differ from a plain program's by a relative error of at most 0.004.
The roundings to bfloat16 on the way count: a program that leaves them out, or rounds other values in their place, can miss the bound.
Values may be sent and summed in bfloat16 or wider, within the bound.
A program may use at most 64 MiB of HBM per device.

v0:
```python
import jax
import jax.numpy as jnp
from jax import lax
from jax.sharding import PartitionSpec as P


def from_behind(value, axis, steps):
    count = lax.axis_size(axis)
    pairs = [(source, (source + steps) % count) for source in range(count)]
    return lax.ppermute(value, axis, pairs)


def on_device(rhs, schur, local_inverse, basis, coarse_inverse, primal_index, neighbour_dof):
    link_table = neighbour_dof[0]
    face_size = link_table.shape[0] // 4
    cases = rhs.shape[2]
    offsets = (face_size, 0, 3 * face_size, 2 * face_size)
    places = []
    for number in range(4):
        places.append(link_table[number * face_size : (number + 1) * face_size] - offsets[number])
    schur_own = schur[0]
    inverse_own = local_inverse[0]
    basis_own = basis[0]
    index_own = primal_index[0]
    column_width = coarse_inverse.shape[1]
    column_base = lax.axis_index("col") * column_width

    def combine(field, incoming):
        collected = [
            jnp.take(incoming[number].astype(jnp.float32), places[number], axis=0)
            for number in range(4)
        ]
        return field + jnp.concatenate(collected, axis=0)

    def assemble(field):
        from_below = from_behind(field[face_size : 2 * face_size], "sub", 1)
        from_above = from_behind(field[:face_size], "sub", -1)
        from_left = from_behind(field[3 * face_size :].astype(jnp.bfloat16), "col", 1).astype(
            jnp.float32
        )
        from_right = from_behind(field[2 * face_size : 3 * face_size], "col", -1)
        return combine(field, (from_below, from_above, from_left, from_right))

    def inner(left_field, right_field):
        return lax.psum(0.5 * jnp.sum(left_field * right_field, axis=0), ("sub", "col"))

    residual = assemble(rhs[0].astype(jnp.float32))
    weighted = (residual * 0.5).astype(jnp.bfloat16)
    local_part = jnp.dot(inverse_own, weighted, preferred_element_type=jnp.float32)
    coarse_load = jnp.dot(basis_own, weighted, preferred_element_type=jnp.float32).astype(
        jnp.bfloat16
    )
    start_block = jnp.zeros((column_width, cases), jnp.bfloat16)
    values = lax.all_gather(coarse_load, ("sub", "col"), axis=0, tiled=True)
    indices = lax.all_gather(index_own, ("sub", "col"), axis=0, tiled=True)
    spots = indices - column_base
    spots = jnp.where((spots >= 0) & (spots < column_width), spots, column_width)
    column_part = start_block.at[spots].set(values, mode="drop")
    partial_rows = jnp.dot(coarse_inverse, column_part, preferred_element_type=jnp.float32)
    start_taken = jnp.zeros((index_own.shape[0], cases), jnp.bfloat16)
    block_rows = lax.psum(partial_rows, "col").astype(jnp.bfloat16)
    piece = lax.all_gather(block_rows, "sub", axis=0, tiled=True)
    spots = index_own
    count = piece.shape[0]
    valid = (spots >= 0) & (spots < count)
    rows = jnp.take(piece, jnp.clip(spots, 0, count - 1), axis=0)
    taken = jnp.where(valid[:, None], rows, start_taken)
    correction = lax.dot_general(
        basis_own, taken, (((0,), (0,)), ((), ())), preferred_element_type=jnp.float32
    )
    first = assemble((local_part + correction) * 0.5)
    rz_first = inner(residual, first)
    image = assemble(
        jnp.dot(schur_own, first.astype(jnp.bfloat16), preferred_element_type=jnp.float32)
    )
    alpha = rz_first / inner(first, image)
    return (alpha * first).astype(jnp.bfloat16)[None]


def solution(mesh):
    return jax.shard_map(
        on_device,
        mesh=mesh,
        in_specs=(
            P(("sub", "col"), None, None),
            P(("sub", "col"), None, None),
            P(("sub", "col"), None, None),
            P(("sub", "col"), None, None),
            P("sub", "col"),
            P(("sub", "col"), None),
            P(("sub", "col"), None),
        ),
        out_specs=P(("sub", "col"), None, None),
        check_vma=False,
    )
```

profile of v0, /device:TPU:0, one launch (start us, length us, event | category | flops | bytes accessed | tf_op | source)
XLA Modules:
  0.0 225.9 jit_solution(8289083633915082191)
XLA Ops:
  0.0 1.2 copy.8
  1.3 3.1 %collective-permute-start = (f32[256,128]{0,1:T(8,128)S(1)}, f32[256,128]{0,1:T(8,128)S(1)}, u32[]{:S(2)}, u32[]{:S(2)}) collective-permute-start(f32[256,128]{0,1:T(8,128)S(1)} %get-tuple-element.16), channel_id=1, source_target_pairs={{0,4},{4,8},{8,12},{12,16},{16,20},{20,24},{24,28},{28,0},{1,5},{5... | collective-permute-start | bytes 393224 | tf_op jit(solution)/shard_map/ppermute | solution.py:10
  4.4 3.1 %collective-permute-start.1 = (f32[256,128]{0,1:T(8,128)S(1)}, f32[256,128]{0,1:T(8,128)S(1)}, u32[]{:S(2)}, u32[]{:S(2)}) collective-permute-start(f32[256,128]{0,1:T(8,128)S(1)} %get-tuple-element.17), channel_id=1, source_target_pairs={{0,28},{4,0},{8,4},{12,8},{16,12},{20,16},{24,20},{28,24},{1,29},{... | collective-permute-start | bytes 393224 | tf_op jit(solution)/shard_map/ppermute | solution.py:10
  8.1 0.8 slice_bitcast_fusion.3
  12.6 37.7 %all-reduce = s32[256]{0:T(256)S(1)} all-reduce(s32[256]{0:T(256)S(1)} %bitcast_dynamic-update-slice_fusion), channel_id=2, replica_groups=mesh['sub'=8,'col'=4] {'sub','col'}, use_global_device_ids=true, to_apply=%add | all-reduce | flops 256 | bytes 2048
  51.5 0.7 gather_fusion.3
  52.9 1.2 broadcast_select_fusion.9
  54.3 0.7 gather_fusion.1
  55.2 0.7 gather_fusion.2
  56.2 0.7 gather_fusion.4
  57.4 41.2 %all_gather.10 = bf16[256,128]{1,0:T(8,128)(2,1)S(1)} all-gather(bf16[8,128]{1,0:T(8,128)(2,1)S(1)} %fusion.9), channel_id=1, replica_groups=mesh['sub'=8,'col'=4] {'sub','col'}, dimensions={0}, use_global_device_ids=true | all-gather | bytes 67584 | tf_op jit(solution)/shard_map/all_gather | solution.py:54
  98.6 1.3 scatter_custom_fusion
  100.0 10.3 %psum.21 = bf16[32,128]{1,0:T(8,128)(2,1)S(1)} all-reduce(f32[32,128]{1,0:T(8,128)S(1)} %convolution_bitcast_fusion), channel_id=1, replica_groups=mesh['sub'=8,'col'=4] {'col'}, use_global_device_ids=true, to_apply=%region_1.3 | all-reduce | flops 4096 | bytes 24576 | tf_op jit(solution)/shard_map/psum | solution.py:61
  110.4 30.5 %all_gather.11 = bf16[256,128]{1,0:T(8,128)(2,1)S(1)} all-gather(bf16[32,128]{1,0:T(8,128)(2,1)S(1)} %psum.21), channel_id=1, replica_groups=mesh['sub'=8,'col'=4] {'sub'}, dimensions={0}, use_global_device_ids=true | all-gather | bytes 73728 | tf_op jit(solution)/shard_map/all_gather | solution.py:62
  140.9 1.6 fusion.2
  143.2 1.4 fusion.8
  144.6 0.8 fusion.34
  146.7 4.7 %collective-permute-start.5 = (f32[256,128]{0,1:T(8,128)}, f32[256,128]{0,1:T(8,128)S(1)}, u32[]{:S(2)}, u32[]{:S(2)}) collective-permute-start(f32[256,128]{0,1:T(8,128)} %get-tuple-element.15), channel_id=1, source_target_pairs={{0,28},{4,0},{8,4},{12,8},{16,12},{20,16},{24,20},{28,24},{1,29},{... | collective-permute-start | bytes 393224 | tf_op jit(solution)/shard_map/ppermute | solution.py:10
  151.9 1.3 broadcast_select_fusion.8
  153.3 2.2 collective-permute-done.6
  155.5 0.7 gather_fusion.7
  156.5 0.7 gather_fusion.5
  157.4 0.7 gather_fusion.6
  158.3 1.0 copy.22
  159.3 0.7 gather_fusion.8
  160.1 0.8 broadcast_select_fusion.6
  161.0 0.7 broadcast_select_fusion.4
  161.8 0.8 fusion.4
  162.7 0.8 fusion.33
  163.4 2.0 collective-permute-start.9
  165.5 1.4 collective-permute-start.11
  166.9 0.9 copy.28
  167.8 1.3 gather_fusion.11
  169.2 1.0 copy.29
  170.2 1.2 broadcast_select_fusion.1
  171.4 1.0 copy.26
  172.4 1.4 gather_fusion.10
  173.8 1.0 copy.27
  174.8 1.3 broadcast_select_fusion.2
  176.1 1.0 copy.24
  177.1 1.3 gather_fusion.9
  178.5 1.0 copy.25
  180.1 1.0 copy.30
  181.1 1.3 gather_fusion.12
  182.5 1.0 copy.31
  183.5 1.5 fusion.15
  185.0 39.9 %all-reduce.1 = (f32[128]{0:T(128)S(1)}, f32[128]{0:T(128)S(1)}) all-reduce(f32[128]{0:T(128)S(1)} %broadcast_multiply_fusion.1, f32[128]{0:T(128)S(1)} %broadcast_multiply_fusion), channel_id=1, replica_groups=mesh['sub'=8,'col'=4] {'sub','col'}, use_global_device_ids=true, to_apply=%region_3.5 | all-reduce | flops 256 | bytes 2048 | tf_op jit(solution)/shard_map/psum | solution.py:45
  225.1 0.8 copy.32
  (100 shorter events, 11.3 us)
Async XLA Ops:
  0.0 140.9 %copy-start = (bf16[1,1024,1024]{2,1,0:T(8,128)(2,1)S(1)}, bf16[1,1024,1024]{2,1,0:T(8,128)(2,1)}, u32[]{:S(2)}) copy-start(bf16[1,1024,1024]{2,1,0:T(8,128)(2,1)} %param.11) | copy-start | bytes 6291460
  0.0 9.0 %copy-start.9 = (s32[1,1024]{1,0:T(1,128)S(1)}, s32[1,1024]{1,0:T(1,128)}, u32[]{:S(2)}) copy-start(s32[1,1024]{1,0:T(1,128)} %param.15) | copy-start | bytes 12292
  0.0 11.2 %copy-start.12 = (s32[1,8]{1,0:T(1,128)S(1)}, s32[1,8]{1,0:T(1,128)}, u32[]{:S(2)}) copy-start(s32[1,8]{1,0:T(1,128)} %param.14) | copy-start | bytes 100
  1.3 52.8 %collective-permute-start = (f32[256,128]{0,1:T(8,128)S(1)}, f32[256,128]{0,1:T(8,128)S(1)}, u32[]{:S(2)}, u32[]{:S(2)}) collective-permute-start(f32[256,128]{0,1:T(8,128)S(1)} %get-tuple-element.16), channel_id=1, source_target_pairs={{0,4},{4,8},{8,12},{12,16},{16,20},{20,24},{24,28},{28,0},{1,5},{5... | collective-permute-start | bytes 393224 | tf_op jit(solution)/shard_map/ppermute | solution.py:10
  4.4 50.7 %collective-permute-start.1 = (f32[256,128]{0,1:T(8,128)S(1)}, f32[256,128]{0,1:T(8,128)S(1)}, u32[]{:S(2)}, u32[]{:S(2)}) collective-permute-start(f32[256,128]{0,1:T(8,128)S(1)} %get-tuple-element.17), channel_id=1, source_target_pairs={{0,28},{4,0},{8,4},{12,8},{16,12},{20,16},{24,20},{28,24},{1,29},{... | collective-permute-start | bytes 393224 | tf_op jit(solution)/shard_map/ppermute | solution.py:10
  7.5 48.6 %collective-permute-start.3 = (f32[256,128]{0,1:T(8,128)S(1)}, f32[256,128]{0,1:T(8,128)S(1)}, u32[]{:S(2)}, u32[]{:S(2)}) collective-permute-start(f32[256,128]{0,1:T(8,128)S(1)} %get-tuple-element.18), channel_id=1, source_target_pairs={{0,3},{1,0},{2,1},{3,2},{4,7},{5,4},{6,5},{7,6},{8,11},{9,8},{10,9... | collective-permute-start | bytes 393224 | tf_op jit(solution)/shard_map/ppermute | solution.py:10
  9.0 42.5 %collective-permute-start.2 = (bf16[256,128]{1,0:T(8,128)(2,1)S(1)}, bf16[256,128]{1,0:T(8,128)(2,1)S(1)}, u32[]{:S(2)}, u32[]{:S(2)}) collective-permute-start(bf16[256,128]{1,0:T(8,128)(2,1)S(1)} %slice_bitcast_fusion.3), channel_id=1, source_target_pairs={{0,1},{1,2},{2,3},{3,0},{4,5},{5,6},{6,7},{7,4},{8,9},{9,10},{10,1... | collective-permute-start | bytes 196616 | tf_op jit(solution)/shard_map/ppermute | solution.py:10
  55.0 2.0 copy-start.6
  55.0 2.1 copy-start.8
  55.0 2.1 copy-start.4
  56.0 1.3 copy-start.2
  56.0 43.9 %copy-start.3 = (bf16[32,64]{1,0:T(8,128)(2,1)S(1)}, bf16[32,64]{1,0:T(8,128)(2,1)}, u32[]{:S(2)}) copy-start(bf16[32,64]{1,0:T(8,128)(2,1)} %param.13) | copy-start | bytes 12292
  57.1 86.1 %copy-start.10 = (pred[8]{0:T(512)(128)(4,1)S(1)}, pred[8]{0:T(512)(128)(4,1)}, u32[]{:S(2)}) copy-start(pred[8]{0:T(512)(128)(4,1)} %and_bitcast_fusion) | copy-start | bytes 28
  57.1 86.1 %copy-start.11 = (pred[8]{0:T(512)(128)(4,1)S(1)}, pred[8]{0:T(512)(128)(4,1)}, u32[]{:S(2)}) copy-start(pred[8]{0:T(512)(128)(4,1)} %compare_and_fusion.4) | copy-start | bytes 28
  146.7 9.7 %collective-permute-start.4 = (f32[256,128]{0,1:T(8,128)}, f32[256,128]{0,1:T(8,128)S(1)}, u32[]{:S(2)}, u32[]{:S(2)}) collective-permute-start(f32[256,128]{0,1:T(8,128)} %get-tuple-element.13), channel_id=1, source_target_pairs={{0,4},{4,8},{8,12},{12,16},{16,20},{20,24},{24,28},{28,0},{1,5},{5... | collective-permute-start | bytes 393224 | tf_op jit(solution)/shard_map/ppermute | solution.py:10
  146.7 10.6 %collective-permute-start.5 = (f32[256,128]{0,1:T(8,128)}, f32[256,128]{0,1:T(8,128)S(1)}, u32[]{:S(2)}, u32[]{:S(2)}) collective-permute-start(f32[256,128]{0,1:T(8,128)} %get-tuple-element.15), channel_id=1, source_target_pairs={{0,28},{4,0},{8,4},{12,8},{16,12},{20,16},{24,20},{28,24},{1,29},{... | collective-permute-start | bytes 393224 | tf_op jit(solution)/shard_map/ppermute | solution.py:10
  151.4 6.8 %collective-permute-start.7 = (f32[256,128]{0,1:T(8,128)}, f32[256,128]{0,1:T(8,128)}, u32[]{:S(2)}, u32[]{:S(2)}) collective-permute-start(f32[256,128]{0,1:T(8,128)} %get-tuple-element.14), channel_id=1, source_target_pairs={{0,3},{1,0},{2,1},{3,2},{4,7},{5,4},{6,5},{7,6},{8,11},{9,8},{10,9... | collective-permute-start | bytes 393224 | tf_op jit(solution)/shard_map/ppermute | solution.py:10
  151.4 4.0 %collective-permute-start.6 = (bf16[256,128]{0,1:T(8,128)(2,1)S(1)}, bf16[256,128]{0,1:T(8,128)(2,1)S(1)}, u32[]{:S(2)}, u32[]{:S(2)}) collective-permute-start(bf16[256,128]{0,1:T(8,128)(2,1)S(1)} %slice.134), channel_id=1, source_target_pairs={{0,1},{1,2},{2,3},{3,0},{4,5},{5,6},{6,7},{7,4},{8,9},{9,10},{10,1... | collective-permute-start | bytes 196616 | tf_op jit(solution)/shard_map/ppermute | solution.py:10
  160.1 1.6 copy-start.1
  162.6 4.3 %collective-permute-start.10 = (bf16[256,128]{0,1:T(8,128)(2,1)S(1)}, bf16[256,128]{0,1:T(8,128)(2,1)}, u32[]{:S(2)}, u32[]{:S(2)}) collective-permute-start(bf16[256,128]{0,1:T(8,128)(2,1)S(1)} %slice.133), channel_id=1, source_target_pairs={{0,1},{1,2},{2,3},{3,0},{4,5},{5,6},{6,7},{7,4},{8,9},{9,10},{10,1... | collective-permute-start | bytes 196616 | tf_op jit(solution)/shard_map/ppermute | solution.py:10
  163.4 8.0 %collective-permute-start.9 = (f32[256,128]{0,1:T(8,128)}, f32[256,128]{0,1:T(8,128)}, u32[]{:S(2)}, u32[]{:S(2)}) collective-permute-start(f32[256,128]{0,1:T(8,128)} %get-tuple-element.12), channel_id=1, source_target_pairs={{0,28},{4,0},{8,4},{12,8},{16,12},{20,16},{24,20},{28,24},{1,29},{... | collective-permute-start | bytes 393224 | tf_op jit(solution)/shard_map/ppermute | solution.py:10
  165.4 10.7 %collective-permute-start.8 = (f32[256,128]{0,1:T(8,128)}, f32[256,128]{0,1:T(8,128)}, u32[]{:S(2)}, u32[]{:S(2)}) collective-permute-start(f32[256,128]{0,1:T(8,128)} %get-tuple-element.10), channel_id=1, source_target_pairs={{0,4},{4,8},{8,12},{12,16},{16,20},{20,24},{24,28},{28,0},{1,5},{5... | collective-permute-start | bytes 393224 | tf_op jit(solution)/shard_map/ppermute | solution.py:10
  165.5 14.7 %collective-permute-start.11 = (f32[256,128]{0,1:T(8,128)}, f32[256,128]{0,1:T(8,128)}, u32[]{:S(2)}, u32[]{:S(2)}) collective-permute-start(f32[256,128]{0,1:T(8,128)} %get-tuple-element.11), channel_id=1, source_target_pairs={{0,3},{1,0},{2,1},{3,2},{4,7},{5,4},{6,5},{7,6},{8,11},{9,8},{10,9... | collective-permute-start | bytes 393224 | tf_op jit(solution)/shard_map/ppermute | solution.py:10
  169.2 10.3 %copy-start.7 = (pred[256]{0:T(512)(128)(4,1)S(1)}, pred[256]{0:T(512)(128)(4,1)}, u32[]{:S(2)}) copy-start(pred[256]{0:T(512)(128)(4,1)} %compare_and_fusion.3) | copy-start | bytes 772
  173.8 9.7 %copy-start.5 = (pred[256]{0:T(512)(128)(4,1)S(1)}, pred[256]{0:T(512)(128)(4,1)}, u32[]{:S(2)}) copy-start(pred[256]{0:T(512)(128)(4,1)} %compare_and_fusion) | copy-start | bytes 772
where the time goes:
time: 227 us; the launch traced here: 226 us
  blocking collectives  160 us (70%)
  local copies, waits for them, and re-layouts  28.1 us (12%)
  other arithmetic  15.7 us (7%)
  starting transfers between devices  15.5 us (7%)
  matrix products  4.13 us (2%)
    all_gather x1, blocking collectives, on_device(): values = lax.all_gather(coarse_load, ('sub', 'col'), axis=0, tiled=True)  41.2 us
    psum x1, blocking collectives, inner(): lax.psum(0.5 * jnp.sum(left_field * right_field, axis=0), ('sub', 'col'))  39.9 us
    unnamed x1, blocking collectives  37.7 us
    all_gather x1, blocking collectives, on_device(): piece = lax.all_gather(block_rows, 'sub', axis=0, tiled=True)  30.5 us
    gather x24, local copies, waits for them, and re-layouts, combine(): jnp.take(incoming[number].astype(jnp.float32), places[number], axis=0)  16 us
    ppermute x12, starting transfers between devices, from_behind(): return lax.ppermute(value, axis, pairs)  15.5 us
    psum x1, blocking collectives, on_device(): block_rows = lax.psum(partial_rows, 'col').astype(jnp.bfloat16)  10.3 us
    select_n x14, other arithmetic, combine(): jnp.take(incoming[number].astype(jnp.float32), places[number], axis=0)  8.71 us
  transfers between devices with their start and end apart: 12, of which 1 were waited for; matrix products, arithmetic and copies ran while one was open for 12% of the time, Pallas kernels for 0%

commit v1 on v0

--- a/solution.py
+++ b/solution.py
@@ -59,7 +59,19 @@
     partial_rows = jnp.dot(coarse_inverse, column_part, preferred_element_type=jnp.float32)
     start_taken = jnp.zeros((index_own.shape[0], cases), jnp.bfloat16)
     block_rows = lax.psum(partial_rows, "col").astype(jnp.bfloat16)
-    piece = lax.all_gather(block_rows, "sub", axis=0, tiled=True)
+    z_new = lax.axis_index("sub")
+    found_now = lax.axis_size("sub")
+    local_next, p_next = (found_now, z_new)
+    piece, value_now = (block_rows, 1)
+    while value_now < local_next:
+        trail = []
+        for j in [*range(local_next)]:
+            trail.append((j, j ^ value_now))
+        tmp = lax.ppermute(piece, "sub", trail)
+        val2 = jnp.concatenate([piece, tmp], axis=0)
+        ready = jnp.concatenate([tmp, piece], axis=0)
+        piece = jnp.where(p_next & value_now == 0, val2, ready)
+        value_now = 2 * value_now
     spots = index_own
     count = piece.shape[0]
     valid = (spots >= 0) & (spots < count)

time: 227 us -> 206 us (0.907)
  blocking collectives: 160 us -> 129 us
  waiting for transfers between devices: 2.19 us -> 11.8 us
    all_gather x1 -> x0, blocking collectives: 30.5 us -> none  [on_device(): piece = lax.all_gather(block_rows, 'sub', axis=0, tiled=True)]
    ppermute x0 -> x3, waiting for transfers between devices: none -> 9.21 us  [on_device(): tmp = lax.ppermute(piece, 'sub', trail)]
  transfers between devices with their start and end apart: 12 -> 15, of which waited for: 1 -> 4; matrix products, arithmetic and copies ran while one was open for 12% -> 15% of each run, Pallas kernels for 0% -> 0%
where the time goes in v1:
time: 206 us; the launch traced here: 205 us
  blocking collectives  129 us (63%)
  local copies, waits for them, and re-layouts  28 us (14%)
  other arithmetic  15.7 us (8%)
  starting transfers between devices  15.5 us (8%)
  waiting for transfers between devices  11.8 us (6%)
  matrix products  4.13 us (2%)
    all_gather x1, blocking collectives, on_device(): values = lax.all_gather(coarse_load, ('sub', 'col'), axis=0, tiled=True)  41.2 us
    psum x1, blocking collectives, inner(): lax.psum(0.5 * jnp.sum(left_field * right_field, axis=0), ('sub', 'col'))  40.2 us
    unnamed x1, blocking collectives  37.7 us
    gather x24, local copies, waits for them, and re-layouts, combine(): jnp.take(incoming[number].astype(jnp.float32), places[number], axis=0)  16 us
    ppermute x12, starting transfers between devices, from_behind(): return lax.ppermute(value, axis, pairs)  15.3 us
    psum x1, blocking collectives, on_device(): block_rows = lax.psum(partial_rows, 'col').astype(jnp.bfloat16)  10.3 us
    ppermute x3, waiting for transfers between devices, on_device(): tmp = lax.ppermute(piece, 'sub', trail)  9.21 us
    select_n x14, other arithmetic, combine(): jnp.take(incoming[number].astype(jnp.float32), places[number], axis=0)  8.71 us
  transfers between devices with their start and end apart: 15, of which 4 were waited for; matrix products, arithmetic and copies ran while one was open for 15% of the time, Pallas kernels for 0%

profile of v1, /device:TPU:0, one launch (start us, length us, event | category | flops | bytes accessed | tf_op | source)
XLA Modules:
  0.0 205.2 jit_solution(17697186114356030925)
XLA Ops:
  0.0 1.2 copy.8
  1.3 3.1 %collective-permute-start = (f32[256,128]{0,1:T(8,128)S(1)}, f32[256,128]{0,1:T(8,128)S(1)}, u32[]{:S(2)}, u32[]{:S(2)}) collective-permute-start(f32[256,128]{0,1:T(8,128)S(1)} %get-tuple-element.16), channel_id=1, source_target_pairs={{0,4},{4,8},{8,12},{12,16},{16,20},{20,24},{24,28},{28,0},{1,5},{5... | collective-permute-start | bytes 393224 | tf_op jit(solution)/shard_map/ppermute | solution.py:10
  4.4 3.1 %collective-permute-start.1 = (f32[256,128]{0,1:T(8,128)S(1)}, f32[256,128]{0,1:T(8,128)S(1)}, u32[]{:S(2)}, u32[]{:S(2)}) collective-permute-start(f32[256,128]{0,1:T(8,128)S(1)} %get-tuple-element.17), channel_id=1, source_target_pairs={{0,28},{4,0},{8,4},{12,8},{16,12},{20,16},{24,20},{28,24},{1,29},{... | collective-permute-start | bytes 393224 | tf_op jit(solution)/shard_map/ppermute | solution.py:10
  8.1 0.8 slice_bitcast_fusion.3
  12.5 37.7 %all-reduce = s32[256]{0:T(256)S(1)} all-reduce(s32[256]{0:T(256)S(1)} %bitcast_dynamic-update-slice_fusion), channel_id=2, replica_groups=mesh['sub'=8,'col'=4] {'sub','col'}, use_global_device_ids=true, to_apply=%add | all-reduce | flops 256 | bytes 2048
  51.4 0.7 gather_fusion.3
  52.9 1.3 broadcast_select_fusion.9
  54.4 0.7 gather_fusion.1
  55.3 0.7 gather_fusion.2
  56.3 0.7 gather_fusion.4
  57.5 41.2 %all_gather.7 = bf16[256,128]{1,0:T(8,128)(2,1)S(1)} all-gather(bf16[8,128]{1,0:T(8,128)(2,1)S(1)} %fusion.9), channel_id=1, replica_groups=mesh['sub'=8,'col'=4] {'sub','col'}, dimensions={0}, use_global_device_ids=true | all-gather | bytes 67584 | tf_op jit(solution)/shard_map/all_gather | solution.py:54
  98.7 1.3 scatter_custom_fusion
  100.2 10.3 %psum.21 = bf16[32,128]{1,0:T(8,128)(2,1)S(1)} all-reduce(f32[32,128]{1,0:T(8,128)S(1)} %convolution_bitcast_fusion), channel_id=1, replica_groups=mesh['sub'=8,'col'=4] {'col'}, use_global_device_ids=true, to_apply=%region_1.3 | all-reduce | flops 4096 | bytes 24576 | tf_op jit(solution)/shard_map/psum | solution.py:61
  110.5 1.6 fusion.2
  112.1 2.0 collective-permute-done.4
  114.9 3.1 %collective-permute-done.5 = bf16[64,128]{1,0:T(8,128)(2,1)S(1)} collective-permute-done((bf16[64,128]{1,0:T(8,128)(2,1)S(1)}, bf16[64,128]{1,0:T(8,128)(2,1)S(1)}, u32[]{:S(2)}, u32[]{:S(2)}) %collective-permute-start.5) | collective-permute-done | bytes 16416 | tf_op jit(solution)/shard_map/ppermute | solution.py:70
  118.7 4.1 %collective-permute-done.6 = bf16[128,128]{1,0:T(8,128)(2,1)S(1)} collective-permute-done((bf16[128,128]{1,0:T(8,128)(2,1)S(1)}, bf16[128,128]{1,0:T(8,128)(2,1)S(1)}, u32[]{:S(2)}, u32[]{:S(2)}) %collective-permute-start.6) | collective-permute-done | bytes 32800 | tf_op jit(solution)/shard_map/ppermute | solution.py:70
  123.6 1.4 fusion.8
  125.0 0.7 fusion.34
  125.8 4.7 %collective-permute-start.8 = (f32[256,128]{0,1:T(8,128)}, f32[256,128]{0,1:T(8,128)S(1)}, u32[]{:S(2)}, u32[]{:S(2)}) collective-permute-start(f32[256,128]{0,1:T(8,128)} %get-tuple-element.15), channel_id=1, source_target_pairs={{0,28},{4,0},{8,4},{12,8},{16,12},{20,16},{24,20},{28,24},{1,29},{... | collective-permute-start | bytes 393224 | tf_op jit(solution)/shard_map/ppermute | solution.py:10
  131.0 1.2 broadcast_select_fusion.8
  132.2 2.6 %collective-permute-done.9 = bf16[256,128]{0,1:T(8,128)(2,1)S(1)} collective-permute-done((bf16[256,128]{0,1:T(8,128)(2,1)S(1)}, bf16[256,128]{0,1:T(8,128)(2,1)S(1)}, u32[]{:S(2)}, u32[]{:S(2)}) %collective-permute-start.9) | collective-permute-done | bytes 65568 | tf_op jit(solution)/shard_map/ppermute | solution.py:10
  134.9 0.7 gather_fusion.7
  135.9 0.7 gather_fusion.5
  136.8 0.7 gather_fusion.6
  137.7 1.0 copy.22
  138.7 0.7 gather_fusion.8
  139.5 0.9 broadcast_select_fusion.6
  141.2 0.8 fusion.4
  142.8 1.6 collective-permute-start.12
  144.8 1.2 collective-permute-start.14
  146.0 0.9 copy.28
  147.0 1.3 gather_fusion.11
  148.3 1.0 copy.29
  149.3 1.3 broadcast_select_fusion.1
  150.6 1.0 copy.26
  151.6 1.3 gather_fusion.10
  152.9 1.0 copy.27
  153.9 1.3 broadcast_select_fusion.2
  155.2 1.0 copy.24
  156.2 1.3 gather_fusion.9
  157.6 1.0 copy.25
  159.3 1.0 copy.30
  160.3 1.3 gather_fusion.12
  161.6 1.0 copy.31
  162.6 1.5 fusion.15
  164.1 40.2 %all-reduce.1 = (f32[128]{0:T(128)S(1)}, f32[128]{0:T(128)S(1)}) all-reduce(f32[128]{0:T(128)S(1)} %broadcast_multiply_fusion.1, f32[128]{0:T(128)S(1)} %broadcast_multiply_fusion), channel_id=1, replica_groups=mesh['sub'=8,'col'=4] {'sub','col'}, use_global_device_ids=true, to_apply=%region_3.5 | all-reduce | flops 256 | bytes 2048 | tf_op jit(solution)/shard_map/psum | solution.py:45
  204.4 0.8 copy.32
  (108 shorter events, 13.3 us)
Async XLA Ops:
  0.0 110.5 %copy-start = (bf16[1,1024,1024]{2,1,0:T(8,128)(2,1)S(1)}, bf16[1,1024,1024]{2,1,0:T(8,128)(2,1)}, u32[]{:S(2)}) copy-start(bf16[1,1024,1024]{2,1,0:T(8,128)(2,1)} %param.11) | copy-start | bytes 6291460
  0.0 9.0 %copy-start.9 = (s32[1,1024]{1,0:T(1,128)S(1)}, s32[1,1024]{1,0:T(1,128)}, u32[]{:S(2)}) copy-start(s32[1,1024]{1,0:T(1,128)} %param.15) | copy-start | bytes 12292
  0.0 11.2 %copy-start.12 = (s32[1,8]{1,0:T(1,128)S(1)}, s32[1,8]{1,0:T(1,128)}, u32[]{:S(2)}) copy-start(s32[1,8]{1,0:T(1,128)} %param.14) | copy-start | bytes 100
  1.3 52.9 %collective-permute-start = (f32[256,128]{0,1:T(8,128)S(1)}, f32[256,128]{0,1:T(8,128)S(1)}, u32[]{:S(2)}, u32[]{:S(2)}) collective-permute-start(f32[256,128]{0,1:T(8,128)S(1)} %get-tuple-element.16), channel_id=1, source_target_pairs={{0,4},{4,8},{8,12},{12,16},{16,20},{20,24},{24,28},{28,0},{1,5},{5... | collective-permute-start | bytes 393224 | tf_op jit(solution)/shard_map/ppermute | solution.py:10
  4.4 50.8 %collective-permute-start.1 = (f32[256,128]{0,1:T(8,128)S(1)}, f32[256,128]{0,1:T(8,128)S(1)}, u32[]{:S(2)}, u32[]{:S(2)}) collective-permute-start(f32[256,128]{0,1:T(8,128)S(1)} %get-tuple-element.17), channel_id=1, source_target_pairs={{0,28},{4,0},{8,4},{12,8},{16,12},{20,16},{24,20},{28,24},{1,29},{... | collective-permute-start | bytes 393224 | tf_op jit(solution)/shard_map/ppermute | solution.py:10
  7.5 48.7 %collective-permute-start.3 = (f32[256,128]{0,1:T(8,128)S(1)}, f32[256,128]{0,1:T(8,128)S(1)}, u32[]{:S(2)}, u32[]{:S(2)}) collective-permute-start(f32[256,128]{0,1:T(8,128)S(1)} %get-tuple-element.18), channel_id=1, source_target_pairs={{0,3},{1,0},{2,1},{3,2},{4,7},{5,4},{6,5},{7,6},{8,11},{9,8},{10,9... | collective-permute-start | bytes 393224 | tf_op jit(solution)/shard_map/ppermute | solution.py:10
  9.0 42.4 %collective-permute-start.2 = (bf16[256,128]{1,0:T(8,128)(2,1)S(1)}, bf16[256,128]{1,0:T(8,128)(2,1)S(1)}, u32[]{:S(2)}, u32[]{:S(2)}) collective-permute-start(bf16[256,128]{1,0:T(8,128)(2,1)S(1)} %slice_bitcast_fusion.3), channel_id=1, source_target_pairs={{0,1},{1,2},{2,3},{3,0},{4,5},{5,6},{6,7},{7,4},{8,9},{9,10},{10,1... | collective-permute-start | bytes 196616 | tf_op jit(solution)/shard_map/ppermute | solution.py:10
  55.1 2.0 copy-start.6
  55.1 2.1 %copy-start.8 = (pred[256]{0:T(512)(128)(4,1)S(1)}, pred[256]{0:T(512)(128)(4,1)}, u32[]{:S(2)}) copy-start(pred[256]{0:T(512)(128)(4,1)} %compare_and_fusion.2) | copy-start | bytes 772
  55.1 2.1 %copy-start.4 = (pred[256]{0:T(512)(128)(4,1)S(1)}, pred[256]{0:T(512)(128)(4,1)}, u32[]{:S(2)}) copy-start(pred[256]{0:T(512)(128)(4,1)} %compare_and_fusion) | copy-start | bytes 772
  56.1 1.2 copy-start.2
  56.1 43.9 %copy-start.3 = (bf16[32,64]{1,0:T(8,128)(2,1)S(1)}, bf16[32,64]{1,0:T(8,128)(2,1)}, u32[]{:S(2)}) copy-start(bf16[32,64]{1,0:T(8,128)(2,1)} %param.13) | copy-start | bytes 12292
  57.3 66.2 %copy-start.10 = (pred[8]{0:T(512)(128)(4,1)S(1)}, pred[8]{0:T(512)(128)(4,1)}, u32[]{:S(2)}) copy-start(pred[8]{0:T(512)(128)(4,1)} %and_bitcast_fusion) | copy-start | bytes 28
  57.3 66.2 %copy-start.11 = (pred[8]{0:T(512)(128)(4,1)S(1)}, pred[8]{0:T(512)(128)(4,1)}, u32[]{:S(2)}) copy-start(pred[8]{0:T(512)(128)(4,1)} %compare_and_fusion.4) | copy-start | bytes 28
  110.5 3.7 %collective-permute-start.4 = (bf16[32,128]{1,0:T(8,128)(2,1)S(1)}, bf16[32,128]{1,0:T(8,128)(2,1)S(1)}, u32[]{:S(2)}, u32[]{:S(2)}) collective-permute-start(bf16[32,128]{1,0:T(8,128)(2,1)S(1)} %psum.21), channel_id=1, source_target_pairs={{0,4},{4,0},{8,12},{12,8},{16,20},{20,16},{24,28},{28,24},{1,5},{5... | collective-permute-start | bytes 24584 | tf_op jit(solution)/shard_map/ppermute | solution.py:70
  114.2 3.8 %collective-permute-start.5 = (bf16[64,128]{1,0:T(8,128)(2,1)S(1)}, bf16[64,128]{1,0:T(8,128)(2,1)S(1)}, u32[]{:S(2)}, u32[]{:S(2)}) collective-permute-start(bf16[64,128]{1,0:T(8,128)(2,1)S(1)} %maximum_select_fusion.2), channel_id=1, source_target_pairs={{0,8},{4,12},{8,0},{12,4},{16,24},{20,28},{24,16},{28,20},{1,9},{5... | collective-permute-start | bytes 49160 | tf_op jit(solution)/shard_map/ppermute | solution.py:70
  118.0 4.9 %collective-permute-start.6 = (bf16[128,128]{1,0:T(8,128)(2,1)S(1)}, bf16[128,128]{1,0:T(8,128)(2,1)S(1)}, u32[]{:S(2)}, u32[]{:S(2)}) collective-permute-start(bf16[128,128]{1,0:T(8,128)(2,1)S(1)} %maximum_select_fusion.1), channel_id=1, source_target_pairs={{0,16},{4,20},{8,24},{12,28},{16,0},{20,4},{24,8},{28,12},{1,17},{... | collective-permute-start | bytes 98312 | tf_op jit(solution)/shard_map/ppermute | solution.py:70
  125.7 10.1 %collective-permute-start.7 = (f32[256,128]{0,1:T(8,128)}, f32[256,128]{0,1:T(8,128)S(1)}, u32[]{:S(2)}, u32[]{:S(2)}) collective-permute-start(f32[256,128]{0,1:T(8,128)} %get-tuple-element.13), channel_id=1, source_target_pairs={{0,4},{4,8},{8,12},{12,16},{16,20},{20,24},{24,28},{28,0},{1,5},{5... | collective-permute-start | bytes 393224 | tf_op jit(solution)/shard_map/ppermute | solution.py:10
  125.8 10.9 %collective-permute-start.8 = (f32[256,128]{0,1:T(8,128)}, f32[256,128]{0,1:T(8,128)S(1)}, u32[]{:S(2)}, u32[]{:S(2)}) collective-permute-start(f32[256,128]{0,1:T(8,128)} %get-tuple-element.15), channel_id=1, source_target_pairs={{0,28},{4,0},{8,4},{12,8},{16,12},{20,16},{24,20},{28,24},{1,29},{... | collective-permute-start | bytes 393224 | tf_op jit(solution)/shard_map/ppermute | solution.py:10
  130.5 7.2 %collective-permute-start.10 = (f32[256,128]{0,1:T(8,128)}, f32[256,128]{0,1:T(8,128)}, u32[]{:S(2)}, u32[]{:S(2)}) collective-permute-start(f32[256,128]{0,1:T(8,128)} %get-tuple-element.14), channel_id=1, source_target_pairs={{0,3},{1,0},{2,1},{3,2},{4,7},{5,4},{6,5},{7,6},{8,11},{9,8},{10,9... | collective-permute-start | bytes 393224 | tf_op jit(solution)/shard_map/ppermute | solution.py:10
  130.5 4.3 %collective-permute-start.9 = (bf16[256,128]{0,1:T(8,128)(2,1)S(1)}, bf16[256,128]{0,1:T(8,128)(2,1)S(1)}, u32[]{:S(2)}, u32[]{:S(2)}) collective-permute-start(bf16[256,128]{0,1:T(8,128)(2,1)S(1)} %slice.134), channel_id=1, source_target_pairs={{0,1},{1,2},{2,3},{3,0},{4,5},{5,6},{6,7},{7,4},{8,9},{9,10},{10,1... | collective-permute-start | bytes 196616 | tf_op jit(solution)/shard_map/ppermute | solution.py:10
  139.5 1.6 copy-start.1
  142.0 4.0 %collective-permute-start.13 = (bf16[256,128]{0,1:T(8,128)(2,1)S(1)}, bf16[256,128]{0,1:T(8,128)(2,1)}, u32[]{:S(2)}, u32[]{:S(2)}) collective-permute-start(bf16[256,128]{0,1:T(8,128)(2,1)S(1)} %slice.133), channel_id=1, source_target_pairs={{0,1},{1,2},{2,3},{3,0},{4,5},{5,6},{6,7},{7,4},{8,9},{9,10},{10,1... | collective-permute-start | bytes 196616 | tf_op jit(solution)/shard_map/ppermute | solution.py:10
  142.8 7.8 %collective-permute-start.12 = (f32[256,128]{0,1:T(8,128)}, f32[256,128]{0,1:T(8,128)}, u32[]{:S(2)}, u32[]{:S(2)}) collective-permute-start(f32[256,128]{0,1:T(8,128)} %get-tuple-element.12), channel_id=1, source_target_pairs={{0,28},{4,0},{8,4},{12,8},{16,12},{20,16},{24,20},{28,24},{1,29},{... | collective-permute-start | bytes 393224 | tf_op jit(solution)/shard_map/ppermute | solution.py:10
  144.5 10.8 %collective-permute-start.11 = (f32[256,128]{0,1:T(8,128)}, f32[256,128]{0,1:T(8,128)}, u32[]{:S(2)}, u32[]{:S(2)}) collective-permute-start(f32[256,128]{0,1:T(8,128)} %get-tuple-element.10), channel_id=1, source_target_pairs={{0,4},{4,8},{8,12},{12,16},{16,20},{20,24},{24,28},{28,0},{1,5},{5... | collective-permute-start | bytes 393224 | tf_op jit(solution)/shard_map/ppermute | solution.py:10
  144.8 14.4 %collective-permute-start.14 = (f32[256,128]{0,1:T(8,128)}, f32[256,128]{0,1:T(8,128)}, u32[]{:S(2)}, u32[]{:S(2)}) collective-permute-start(f32[256,128]{0,1:T(8,128)} %get-tuple-element.11), channel_id=1, source_target_pairs={{0,3},{1,0},{2,1},{3,2},{4,7},{5,4},{6,5},{7,6},{8,11},{9,8},{10,9... | collective-permute-start | bytes 393224 | tf_op jit(solution)/shard_map/ppermute | solution.py:10
  148.3 10.3 %copy-start.7 = (pred[256]{0:T(512)(128)(4,1)S(1)}, pred[256]{0:T(512)(128)(4,1)}, u32[]{:S(2)}) copy-start(pred[256]{0:T(512)(128)(4,1)} %compare_and_fusion.3) | copy-start | bytes 772
  152.9 9.7 %copy-start.5 = (pred[256]{0:T(512)(128)(4,1)S(1)}, pred[256]{0:T(512)(128)(4,1)}, u32[]{:S(2)}) copy-start(pred[256]{0:T(512)(128)(4,1)} %compare_and_fusion) | copy-start | bytes 772
